TPU v7x, 256 devices: a whole 4x4x8 slice. The times are simulated.
256 devices in a mesh: rows: 8 (over z_hi, x), lat: 32 (over y, z_lo, core).
Axes of the slice: x: 4, y: 4, z: 8 (z_hi: 2, z_lo: 4; z = z_hi * 4 + z_lo), core: 2. Of those that a mesh axis runs over, the one named last changes fastest.
Arguments:
- residual: bfloat16 [1024, 4608], P('rows', 'lat'), may hold values from -64 to 64
- enc_weight: bfloat16 [4608, 65536], P('rows', 'lat'), may hold values from -0.09375 to 0.09375
- dec_weight: bfloat16 [65536, 4608], P('lat', 'rows'), may hold values from -0.078125 to 0.078125
- enc_bias: float32 [65536], P('lat'), may hold values from -3 to 3
- dec_bias: float32 [4608], P('rows'), may hold values from -3 to 3
- active_blocks: int32 [8, 96], replicated, may hold values from 0 to 511, as said below
- active_counts: int32 [1024], P('rows'), may hold values from 1 to 96, as said below
Outputs:
- latents: bfloat16 [1024, 65536], P('rows', 'lat')
- recon: bfloat16 [1024, 4608], P('lat', 'rows')
Inputs may be any that keep to these rules, and one draw needn't show every extreme that they name: `active_blocks`: each row lists 96 different latent blocks; at most 6 of them lie among the 16 blocks of one index of lat, and exactly 6 for some index in every row. `active_counts`: in every row block some row uses all 96 entries and some row uses one.
All inputs are finite; a program needn't handle non-finite values.
Results may differ from a plain program's by a relative error of at most 0.0058.
Values may be sent and summed in bfloat16 or wider, within the bound.
No kernel may reach another device: no remote copies, remote signals or barrier semaphores. Data moves between devices by JAX's collectives and lax.ppermute only.
A program may use at most 128 MiB of HBM per device.

v0:
```python
import jax
import jax.numpy as jnp
from jax import lax
from jax.sharding import PartitionSpec as P

BLOCK = 128


def shards(residual, enc_weight, dec_weight, enc_bias, dec_bias, active_blocks, active_counts):
    own_rows = residual.shape[0]
    row_count = lax.axis_size("rows")
    tokens_all = own_rows * row_count
    residual_t = residual.T
    full_t = lax.all_gather(residual_t, "lat", axis=0, tiled=True)
    width = full_t.shape[0]
    gram_block = lax.dot_general(
        residual_t, full_t, (((1,), (1,)), ((), ())), preferred_element_type=jnp.float32
    )
    gram_block = lax.psum(gram_block, "rows")
    wide_own = residual_t.astype(jnp.float32)
    energy = lax.psum(jnp.sum(wide_own * wide_own), ("rows", "lat"))
    mean_sq = energy / (tokens_all * width)
    chat = (gram_block / (tokens_all * (mean_sq + 1e-05))).astype(jnp.bfloat16)
    term = lax.dot_general(
        chat, residual_t, (((0,), (0,)), ((), ())), preferred_element_type=jnp.float32
    )
    term = lax.psum(term, "lat")
    white_t = (1.5 * full_t.astype(jnp.float32) - 0.5 * term).astype(jnp.bfloat16)
    shard_width = enc_weight.shape[1]
    pre = lax.dot_general(
        white_t,
        lax.all_gather(enc_weight, "rows", axis=0, tiled=True),
        (((0,), (0,)), ((), ())),
        preferred_element_type=jnp.float32,
    )
    pre = pre + enc_bias
    shard_blocks = shard_width // BLOCK
    own_blocks = own_rows // BLOCK
    listed_count = active_blocks.shape[1]
    lat_index = lax.axis_index("lat")
    row_index = lax.axis_index("rows")
    global_ids = lat_index * shard_blocks + jnp.arange(shard_blocks, dtype=jnp.int32)
    matches = active_blocks[:, :, None] == global_ids[None, None, :]
    slots = jnp.arange(listed_count, dtype=jnp.int32)[None, :, None]
    listed = jnp.any(matches, axis=1)
    slot_rank = jnp.sum(jnp.where(matches, slots, 0), axis=1) + listed_count * (
        1 - listed.astype(jnp.int32)
    )
    own_rank = lax.dynamic_slice_in_dim(slot_rank, row_index * own_blocks, own_blocks, 0)
    live = own_rank[:, None, :] < active_counts.reshape(own_blocks, BLOCK)[:, :, None]
    shaped = jnp.maximum(pre, 0.0).reshape(own_blocks, BLOCK, shard_blocks, BLOCK) * live[
        :, :, :, None
    ].astype(jnp.float32)
    latents = shaped.reshape(own_rows, shard_width).astype(jnp.bfloat16)
    terms = jnp.dot(
        lax.all_gather(latents, "rows", axis=0, tiled=True),
        dec_weight,
        preferred_element_type=jnp.float32,
    )
    recon_part = lax.psum_scatter(terms, "lat", scatter_dimension=0, tiled=True)
    recon = (recon_part + dec_bias).astype(jnp.bfloat16)
    return (latents, recon)


def solution(mesh):
    in_specs = (
        P("rows", "lat"),
        P("rows", "lat"),
        P("lat", "rows"),
        P("lat"),
        P("rows"),
        P(),
        P("rows"),
    )
    out_specs = (P("rows", "lat"), P("lat", "rows"))
    return jax.shard_map(shards, mesh=mesh, in_specs=in_specs, out_specs=out_specs, check_vma=False)
```

profile of v0, /device:TPU:2, one launch (start us, length us, event | category | flops | bytes accessed | tf_op | source)
XLA Modules:
  0.0 1131.7 jit_solution(10821013051532588925)
XLA Ops:
  7.2 0.7 all-gather.4.cloned.1.call-update
  7.9 0.0 all-reduce.3.cloned.1.call-start
  8.0 63.8 %all-gather.4.cloned.1.call-done = bf16[4608,128]{1,0:T(8,128)(2,1)} async-done(((bf16[144,128]{1,0:T(8,128)(2,1)}), bf16[4608,128]{1,0:T(8,128)(2,1)}) %all-gather.4.cloned.1.call-update) | async-done | bytes 1179664 | tf_op jit(solution)/shard_map/all_gather | solution.py:14
  71.7 3.3 fusion.9
  75.1 0.0 all-reduce.5.cloned.1.call-start
  75.1 0.6 multiply_reduce_fusion
  75.7 103.7 %psum.22 = f32[]{:T(128)} all-reduce(f32[]{:T(128)} %multiply_reduce_fusion), channel_id=1, replica_groups=mesh['rows'=8,'lat'=32] {'rows','lat'}, use_global_device_ids=true, to_apply=%region_2.0 | all-reduce | flops 1 | bytes 8 | tf_op jit(solution)/shard_map/psum | solution.py:21
  180.1 45.0 %all-reduce.3.cloned.1.call-done = f32[144,4608]{1,0:T(8,128)} async-done(((f32[144,4608]{1,0:T(8,128)}), f32[144,4608]{1,0:T(8,128)}) %all-reduce.3.cloned.1.call-update) | async-done | bytes 2654224 | tf_op jit(solution)/shard_map/psum | solution.py:19
  225.1 4.1 fusion.3
  229.2 0.0 all-gather.6.cloned.1.call-start
  229.3 0.5 all-gather.6.cloned.1.call-update
  229.9 0.3 compare_reduce_fusion
  230.1 0.3 fusion.6
  230.5 0.7 compare_convert_fusion
  231.2 0.7 copy.9
  231.9 283.2 %all-reduce.5.cloned.1.call-done = f32[4608,128]{1,0:T(8,128)} async-done(((f32[4608,128]{1,0:T(8,128)}), f32[4608,128]{1,0:T(8,128)}) %all-reduce.5.cloned.1.call-update) | async-done | bytes 2359312 | tf_op jit(solution)/shard_map/psum | solution.py:27
  515.1 340.4 %all-gather.6.cloned.1.call-done = bf16[4608,2048]{1,0:T(8,128)(2,1)} async-done(((bf16[576,2048]{1,0:T(8,128)(2,1)}), bf16[4608,2048]{1,0:T(8,128)(2,1)}) %all-gather.6.cloned.1.call-update) | async-done | bytes 18874384 | tf_op jit(solution)/shard_map/all_gather | solution.py:32
  855.5 1.2 mul.45
  856.7 10.7 fusion.2
  867.4 0.0 reduce-scatter.2.cloned.1.call-start
  867.5 101.9 %all-gather.8.cloned.1.call-done = bf16[1024,2048]{1,0:T(8,128)(2,1)} async-done(((bf16[128,2048]{1,0:T(8,128)(2,1)}), bf16[1024,2048]{1,0:T(8,128)(2,1)}) %all-gather.8.cloned.1.call-update) | async-done | bytes 4194320 | tf_op jit(solution)/shard_map/all_gather | solution.py:56
  969.4 7.2 fusion.10
  976.6 146.8 %reduce-scatter.2.cloned.1.call-done = f32[32,576]{1,0:T(8,128)} async-done(((f32[1024,576]{1,0:T(8,128)}), f32[32,576]{1,0:T(8,128)}) %reduce-scatter.2.cloned.1.call-update) | async-done | bytes 73744 | tf_op jit(solution)/shard_map/reduce_scatter | solution.py:60
  1123.3 1.5 add_convert_fusion
  (21 shorter events, 0.2 us)
Async XLA Ops:
  7.2 962.2 %copy-start = (bf16[2048,576]{0,1:T(8,128)(2,1)S(1)}, bf16[2048,576]{0,1:T(8,128)(2,1)}, u32[]{:S(2)}) copy-start(bf16[2048,576]{0,1:T(8,128)(2,1)} %param.9) | copy-start | bytes 7077892
  7.2 64.5 %all-gather.4.cloned.1.call-start = ((), (), s32[]{:S(2)}) async-start(), calls=%async_computation.1 | async-start | bytes 1216512 | tf_op jit(solution)/shard_map/all_gather | solution.py:14
  7.9 67.2 %copy-start.2 = (bf16[128,144]{0,1:T(8,128)(2,1)S(1)}, bf16[128,144]{0,1:T(8,128)(2,1)}, u32[]{:S(2)}) copy-start(bf16[128,144]{0,1:T(8,128)(2,1)} %param.7) | copy-start | bytes 110596
  7.9 217.2 %all-reduce.3.cloned.1.call-start = ((), (), s32[]{:S(2)}) async-start(), calls=%async_computation.2 | async-start | bytes 5308416 | tf_op jit(solution)/shard_map/psum | solution.py:19
  75.1 440.1 %all-reduce.5.cloned.1.call-start = ((), (), s32[]{:S(2)}) async-start(), calls=%async_computation.3 | async-start | bytes 4718592 | tf_op jit(solution)/shard_map/psum | solution.py:27
  229.2 0.7 copy-start.3
  229.2 627.5 %copy-start.1 = (bf16[4608,128]{1,0:T(8,128)(2,1)S(1)}, bf16[4608,128]{1,0:T(8,128)(2,1)}, u32[]{:S(2)}) copy-start(bf16[4608,128]{1,0:T(8,128)(2,1)} %all-gather.4.cloned.1.call-done) | copy-start | bytes 3538948
  229.2 627.5 %copy-start.4 = (f32[2048]{0:T(1024)S(1)}, f32[2048]{0:T(1024)}, u32[]{:S(2)}) copy-start(f32[2048]{0:T(1024)} %param.10) | copy-start | bytes 24580
  229.2 626.3 %all-gather.6.cloned.1.call-start = ((), (), s32[]{:S(2)}) async-start(), calls=%async_computation.4 | async-start | bytes 21233664 | tf_op jit(solution)/shard_map/all_gather | solution.py:32
  229.8 739.6 %all-gather.8.cloned.1.call-start = ((), (), s32[]{:S(2)}) async-start(), calls=%async_computation.5 | async-start | bytes 4718592 | tf_op jit(solution)/shard_map/all_gather | solution.py:56
  867.4 255.9 %reduce-scatter.2.cloned.1.call-start = ((), (), s32[]{:S(2)}) async-start(), calls=%async_computation.6 | async-start | bytes 2703360 | tf_op jit(solution)/shard_map/reduce_scatter | solution.py:60
  976.5 146.8 %copy-start.5 = (f32[576]{0:T(1024)S(1)}, f32[576]{0:T(1024)}, u32[]{:S(2)}) copy-start(f32[576]{0:T(1024)} %param.11) | copy-start | bytes 6916
Sparse Core Ops, SparseCore 0:
  9.8 61.8 all-gather.3
  75.2 149.8 all-reduce.2
  229.3 285.7 all-reduce.4
  517.6 337.8 all-gather.5
  867.6 101.7 all-gather.7
  976.7 146.6 reduce-scatter.1
where the time goes:
time: 1130 us
  waiting for transfers between devices  982 us (87%)
  blocking collectives  104 us (9%)
  matrix products  25.3 us (2%)
  between operations  14.9 us (1%)
    all_gather x1, waiting for transfers between devices, shards(): lax.all_gather(enc_weight, 'rows', axis=0, tiled=True)  340 us
    psum x1, waiting for transfers between devices, shards(): term = lax.psum(term, 'lat')  283 us
    reduce_scatter x1, waiting for transfers between devices, shards(): recon_part = lax.psum_scatter(terms, 'lat', scatter_dimension=0, tiled=True)  147 us
    psum x1, blocking collectives, shards(): energy = lax.psum(jnp.sum(wide_own * wide_own), ('rows', 'lat'))  104 us
    all_gather x1, waiting for transfers between devices, shards(): lax.all_gather(latents, 'rows', axis=0, tiled=True)  102 us
    all_gather x1, waiting for transfers between devices, shards(): full_t = lax.all_gather(residual_t, 'lat', axis=0, tiled=True)  63.8 us
    psum x1, waiting for transfers between devices, shards(): gram_block = lax.psum(gram_block, 'rows')  45 us
  transfers between devices with their start and end apart: 6, of which 6 were waited for; matrix products, arithmetic and copies ran while one was open for 0% of the time, Pallas kernels for 0%

commit v1 on v0

--- a/solution.py
+++ b/solution.py
@@ -24,7 +24,8 @@
     term = lax.dot_general(
         chat, residual_t, (((0,), (0,)), ((), ())), preferred_element_type=jnp.float32
     )
-    term = lax.psum(term, "lat")
+    meet_masks = lambda content, mesh_name: jnp.sum(jax.lax.all_gather(content, mesh_name), axis=0)
+    term = meet_masks(term, "lat")
     white_t = (1.5 * full_t.astype(jnp.float32) - 0.5 * term).astype(jnp.bfloat16)
     shard_width = enc_weight.shape[1]
     pre = lax.dot_general(

time: 1130 us -> 1240 us (1.097)
  waiting for transfers between devices: 982 us -> 1070 us
  other arithmetic: 3.43 us -> 29.8 us
    all_gather x0 -> x1, waiting for transfers between devices: none -> 394 us  [shards(): jax.lax.all_gather(content, mesh_name)]
    psum x1 -> x0, waiting for transfers between devices: 283 us -> none  [shards(): term = lax.psum(term, 'lat')]
    reduce_sum x0 -> x1, other arithmetic: none -> 27 us  [shards(): jnp.sum(jax.lax.all_gather(content, mesh_name), axis=0)]
    all_gather x1, waiting for transfers between devices: 340 us -> 315 us  [shards(): lax.all_gather(enc_weight, 'rows', axis=0, tiled=True)]
  transfers between devices with their start and end apart: 6 -> 6, of which waited for: 6 -> 6; matrix products, arithmetic and copies ran while one was open for 0% -> 2% of each run, Pallas kernels for 0% -> 0%
where the time goes in v1:
time: 1240 us
  waiting for transfers between devices  1070 us (86%)
  blocking collectives  104 us (8%)
  other arithmetic  29.8 us (2%)
  matrix products  25.3 us (2%)
  between operations  14.8 us (1%)
    all_gather x1, waiting for transfers between devices, shards(): jax.lax.all_gather(content, mesh_name)  394 us
    all_gather x1, waiting for transfers between devices, shards(): lax.all_gather(enc_weight, 'rows', axis=0, tiled=True)  315 us
    reduce_scatter x1, waiting for transfers between devices, shards(): recon_part = lax.psum_scatter(terms, 'lat', scatter_dimension=0, tiled=True)  146 us
    psum x1, blocking collectives, shards(): energy = lax.psum(jnp.sum(wide_own * wide_own), ('rows', 'lat'))  104 us
    all_gather x1, waiting for transfers between devices, shards(): lax.all_gather(latents, 'rows', axis=0, tiled=True)  102 us
    all_gather x1, waiting for transfers between devices, shards(): full_t = lax.all_gather(residual_t, 'lat', axis=0, tiled=True)  63.8 us
    psum x1, waiting for transfers between devices, shards(): gram_block = lax.psum(gram_block, 'rows')  45 us
    reduce_sum x1, other arithmetic, shards(): jnp.sum(jax.lax.all_gather(content, mesh_name), axis=0)  27 us
  transfers between devices with their start and end apart: 6, of which 6 were waited for; matrix products, arithmetic and copies ran while one was open for 2% of the time, Pallas kernels for 0%

profile of v1, /device:TPU:2, one launch (start us, length us, event | category | flops | bytes accessed | tf_op | source)
XLA Modules:
  0.0 1243.2 jit_solution(15043988740901542591)
XLA Ops:
  7.2 0.7 all-gather.6.cloned.1.call-update
  8.0 63.8 %all-gather.6.cloned.1.call-done = bf16[4608,128]{1,0:T(8,128)(2,1)} async-done(((bf16[144,128]{1,0:T(8,128)(2,1)}), bf16[4608,128]{1,0:T(8,128)(2,1)}) %all-gather.6.cloned.1.call-update) | async-done | bytes 1179664 | tf_op jit(solution)/shard_map/all_gather | solution.py:14
  71.7 3.3 fusion.9
  75.1 0.0 all-gather.12.cloned.1.call-start
  75.1 0.6 multiply_reduce_fusion
  75.7 104.4 %psum.15 = f32[]{:T(128)} all-reduce(f32[]{:T(128)} %multiply_reduce_fusion), channel_id=1, replica_groups=mesh['rows'=8,'lat'=32] {'rows','lat'}, use_global_device_ids=true, to_apply=%region_2.0 | all-reduce | flops 1 | bytes 8 | tf_op jit(solution)/shard_map/psum | solution.py:21
  180.8 45.0 %all-reduce.2.cloned.1.call-done = f32[144,4608]{1,0:T(8,128)} async-done(((f32[144,4608]{1,0:T(8,128)}), f32[144,4608]{1,0:T(8,128)}) %all-reduce.2.cloned.1.call-update) | async-done | bytes 2654224 | tf_op jit(solution)/shard_map/psum | solution.py:19
  225.7 4.0 fusion.3
  229.8 0.0 all-gather.8.cloned.1.call-start
  229.9 0.5 all-gather.8.cloned.1.call-update
  230.5 0.3 compare_reduce_fusion
  230.8 0.3 fusion.6
  231.1 0.1 compare_convert_fusion
  231.2 0.7 copy.9
  231.9 393.8 %all-gather.12.cloned.1.call-done = f32[147456,128]{1,0:T(8,128)} async-done(((f32[4608,128]{1,0:T(8,128)}), f32[147456,128]{1,0:T(8,128)}) %all-gather.12.cloned.1.call-update) | async-done | bytes 75497488 | tf_op jit(solution)/shard_map/all_gather | solution.py:27
  625.7 27.0 %reduce_sum.28 = f32[4608,128]{1,0:T(8,128)} reduce(f32[32,4608,128]{2,1,0:T(8,128)} %bitcast.1, f32[]{:T(128)} %constant.4.clone.1), dimensions={0}, to_apply=%region_3.0 | reduce | flops 18284544 | bytes 77856768 | tf_op jit(solution)/shard_map/reduce_sum | solution.py:27
  652.7 315.1 %all-gather.8.cloned.1.call-done = bf16[4608,2048]{1,0:T(8,128)(2,1)} async-done(((bf16[576,2048]{1,0:T(8,128)(2,1)}), bf16[4608,2048]{1,0:T(8,128)(2,1)}) %all-gather.8.cloned.1.call-update) | async-done | bytes 18874384 | tf_op jit(solution)/shard_map/all_gather | solution.py:33
  967.8 1.2 mul.45
  969.0 10.7 fusion.2
  979.7 0.0 reduce-scatter.2.cloned.1.call-start
  979.8 101.9 %all-gather.10.cloned.1.call-done = bf16[1024,2048]{1,0:T(8,128)(2,1)} async-done(((bf16[128,2048]{1,0:T(8,128)(2,1)}), bf16[1024,2048]{1,0:T(8,128)(2,1)}) %all-gather.10.cloned.1.call-update) | async-done | bytes 4194320 | tf_op jit(solution)/shard_map/all_gather | solution.py:57
  1081.7 7.2 fusion.10
  1088.9 146.0 %reduce-scatter.2.cloned.1.call-done = f32[32,576]{1,0:T(8,128)} async-done(((f32[1024,576]{1,0:T(8,128)}), f32[32,576]{1,0:T(8,128)}) %reduce-scatter.2.cloned.1.call-update) | async-done | bytes 73744 | tf_op jit(solution)/shard_map/reduce_scatter | solution.py:61
  1234.9 1.5 add_convert_fusion
  (24 shorter events, 0.2 us)
Async XLA Ops:
  7.2 1074.5 %copy-start = (bf16[2048,576]{0,1:T(8,128)(2,1)S(1)}, bf16[2048,576]{0,1:T(8,128)(2,1)}, u32[]{:S(2)}) copy-start(bf16[2048,576]{0,1:T(8,128)(2,1)} %param.9) | copy-start | bytes 7077892
  7.2 64.5 %all-gather.6.cloned.1.call-start = ((), (), s32[]{:S(2)}) async-start(), calls=%async_computation.1 | async-start | bytes 1216512 | tf_op jit(solution)/shard_map/all_gather | solution.py:14
  7.9 67.2 %copy-start.2 = (bf16[128,144]{0,1:T(8,128)(2,1)S(1)}, bf16[128,144]{0,1:T(8,128)(2,1)}, u32[]{:S(2)}) copy-start(bf16[128,144]{0,1:T(8,128)(2,1)} %param.7) | copy-start | bytes 110596
  7.9 217.8 %all-reduce.2.cloned.1.call-start = ((), (), s32[]{:S(2)}) async-start(), calls=%async_computation.2 | async-start | bytes 5308416 | tf_op jit(solution)/shard_map/psum | solution.py:19
  75.1 550.7 %all-gather.12.cloned.1.call-start = ((), (), s32[]{:S(2)}) async-start(), calls=%async_computation.6 | async-start | bytes 77856768 | tf_op jit(solution)/shard_map/all_gather | solution.py:27
  229.8 0.7 copy-start.3
  229.8 1.3 copy-start.6
  229.8 738.0 %all-gather.8.cloned.1.call-start = ((), (), s32[]{:S(2)}) async-start(), calls=%async_computation.3 | async-start | bytes 21233664 | tf_op jit(solution)/shard_map/all_gather | solution.py:33
  230.4 851.3 %all-gather.10.cloned.1.call-start = ((), (), s32[]{:S(2)}) async-start(), calls=%async_computation.4 | async-start | bytes 4718592 | tf_op jit(solution)/shard_map/all_gather | solution.py:57
  625.7 343.3 %copy-start.1 = (bf16[4608,128]{1,0:T(8,128)(2,1)S(1)}, bf16[4608,128]{1,0:T(8,128)(2,1)}, u32[]{:S(2)}) copy-start(bf16[4608,128]{1,0:T(8,128)(2,1)} %all-gather.6.cloned.1.call-done) | copy-start | bytes 3538948
  625.7 343.3 %copy-start.4 = (f32[2048]{0:T(1024)S(1)}, f32[2048]{0:T(1024)}, u32[]{:S(2)}) copy-start(f32[2048]{0:T(1024)} %param.10) | copy-start | bytes 24580
  979.7 255.1 %reduce-scatter.2.cloned.1.call-start = ((), (), s32[]{:S(2)}) async-start(), calls=%async_computation.5 | async-start | bytes 2703360 | tf_op jit(solution)/shard_map/reduce_scatter | solution.py:61
  1088.8 146.0 %copy-start.5 = (f32[576]{0:T(1024)S(1)}, f32[576]{0:T(1024)}, u32[]{:S(2)}) copy-start(f32[576]{0:T(1024)} %param.11) | copy-start | bytes 6916
Sparse Core Ops, SparseCore 0:
  9.8 61.8 all-gather.5
  75.2 150.5 all-reduce.1
  229.9 395.7 all-gather.11
  628.2 339.5 all-gather.7
  979.9 101.7 all-gather.9
  1089.0 145.8 reduce-scatter.1

commit v2 on v0

--- a/solution.py
+++ b/solution.py
@@ -4,6 +4,13 @@
 from jax.sharding import PartitionSpec as P
 
 BLOCK = 128
+
+
+def all_by_exchange(shard, axis, dim):
+    devices = lax.axis_size(axis)
+    blocks = jnp.stack([shard for _ in range(devices)])
+    blocks = lax.all_to_all(blocks, axis, split_axis=0, concat_axis=0)
+    return jnp.concatenate(blocks, axis=dim)
 
 
 def shards(residual, enc_weight, dec_weight, enc_bias, dec_bias, active_blocks, active_counts):
@@ -29,7 +36,7 @@
     shard_width = enc_weight.shape[1]
     pre = lax.dot_general(
         white_t,
-        lax.all_gather(enc_weight, "rows", axis=0, tiled=True),
+        all_by_exchange(enc_weight, "rows", 0),
         (((0,), (0,)), ((), ())),
         preferred_element_type=jnp.float32,
     )

time: 1130 us -> 1200 us (1.062)
  waiting for transfers between devices: 982 us -> 1020 us
    all_gather x1, waiting for transfers between devices: 63.8 us -> 443 us  [shards(): full_t = lax.all_gather(residual_t, 'lat', axis=0, tiled=True)]
    all_gather x1 -> x0, waiting for transfers between devices: 340 us -> none  [shards(): lax.all_gather(enc_weight, 'rows', axis=0, tiled=True)]
  transfers between devices with their start and end apart: 6 -> 6, of which waited for: 6 -> 5; matrix products, arithmetic and copies ran while one was open for 0% -> 1% of each run, Pallas kernels for 0% -> 0%
where the time goes in v2:
time: 1200 us
  waiting for transfers between devices  1020 us (85%)
  blocking collectives  111 us (9%)
  matrix products  25.2 us (2%)
  between operations  14.5 us (1%)
    all_gather x1, waiting for transfers between devices, shards(): full_t = lax.all_gather(residual_t, 'lat', axis=0, tiled=True)  443 us
    psum x1, waiting for transfers between devices, shards(): term = lax.psum(term, 'lat')  284 us
    reduce_scatter x1, waiting for transfers between devices, shards(): recon_part = lax.psum_scatter(terms, 'lat', scatter_dimension=0, tiled=True)  147 us
    psum x1, blocking collectives, shards(): energy = lax.psum(jnp.sum(wide_own * wide_own), ('rows', 'lat'))  111 us
    all_gather x1, waiting for transfers between devices, shards(): lax.all_gather(latents, 'rows', axis=0, tiled=True)  105 us
    psum x1, waiting for transfers between devices, shards(): gram_block = lax.psum(gram_block, 'rows')  42.7 us
  transfers between devices with their start and end apart: 6, of which 5 were waited for; matrix products, arithmetic and copies ran while one was open for 1% of the time, Pallas kernels for 0%

profile of v2, /device:TPU:2, one launch (start us, length us, event | category | flops | bytes accessed | tf_op | source)
XLA Modules:
  0.0 1198.7 jit_solution(5023443767466472331)
XLA Ops:
  7.2 7.9 stack.2
  15.1 11.6 all-to-all-start
  26.7 0.7 all-gather.3.cloned.1.call-update
  27.4 443.4 %all-gather.3.cloned.1.call-done = bf16[4608,128]{1,0:T(8,128)(2,1)} async-done(((bf16[144,128]{1,0:T(8,128)(2,1)}), bf16[4608,128]{1,0:T(8,128)(2,1)}) %all-gather.3.cloned.1.call-update) | async-done | bytes 1179664 | tf_op jit(solution)/shard_map/all_gather | solution.py:21
  470.8 3.3 fusion.9
  474.1 0.0 all-reduce.5.cloned.1.call-start
  474.1 0.6 multiply_reduce_fusion
  474.8 110.9 %psum.22 = f32[]{:T(128)} all-reduce(f32[]{:T(128)} %multiply_reduce_fusion), channel_id=1, replica_groups=mesh['rows'=8,'lat'=32] {'rows','lat'}, use_global_device_ids=true, to_apply=%region_2.0 | all-reduce | flops 1 | bytes 8 | tf_op jit(solution)/shard_map/psum | solution.py:28
  586.3 42.7 %all-reduce.3.cloned.1.call-done = f32[144,4608]{1,0:T(8,128)} async-done(((f32[144,4608]{1,0:T(8,128)}), f32[144,4608]{1,0:T(8,128)}) %all-reduce.3.cloned.1.call-update) | async-done | bytes 2654224 | tf_op jit(solution)/shard_map/psum | solution.py:26
  629.0 4.1 fusion.3
  633.1 0.0 all-gather.5.cloned.1.call-start
  633.2 0.6 copy-done.3
  633.8 0.3 compare_reduce_fusion
  634.0 0.3 fusion.6
  634.4 0.7 compare_convert_fusion
  635.1 0.7 copy.9
  635.8 284.3 %all-reduce.5.cloned.1.call-done = f32[4608,128]{1,0:T(8,128)} async-done(((f32[4608,128]{1,0:T(8,128)}), f32[4608,128]{1,0:T(8,128)}) %all-reduce.5.cloned.1.call-update) | async-done | bytes 2359312 | tf_op jit(solution)/shard_map/psum | solution.py:34
  920.2 1.2 mul.45
  921.3 10.7 fusion.2
  932.1 0.0 reduce-scatter.2.cloned.1.call-start
  932.1 104.8 %all-gather.5.cloned.1.call-done = bf16[1024,2048]{1,0:T(8,128)(2,1)} async-done(((bf16[128,2048]{1,0:T(8,128)(2,1)}), bf16[1024,2048]{1,0:T(8,128)(2,1)}) %all-gather.5.cloned.1.call-update) | async-done | bytes 4194320 | tf_op jit(solution)/shard_map/all_gather | solution.py:63
  1036.9 7.2 fusion.10
  1044.1 146.6 %reduce-scatter.2.cloned.1.call-done = f32[32,576]{1,0:T(8,128)} async-done(((f32[1024,576]{1,0:T(8,128)}), f32[32,576]{1,0:T(8,128)}) %reduce-scatter.2.cloned.1.call-update) | async-done | bytes 73744 | tf_op jit(solution)/shard_map/reduce_scatter | solution.py:67
  1190.7 1.5 add_convert_fusion
  (21 shorter events, 0.2 us)
Async XLA Ops:
  7.2 1029.8 %copy-start = (bf16[2048,576]{0,1:T(8,128)(2,1)S(1)}, bf16[2048,576]{0,1:T(8,128)(2,1)}, u32[]{:S(2)}) copy-start(bf16[2048,576]{0,1:T(8,128)(2,1)} %param.9) | copy-start | bytes 7077892
  15.1 455.7 %copy-start.2 = (bf16[128,144]{0,1:T(8,128)(2,1)S(1)}, bf16[128,144]{0,1:T(8,128)(2,1)}, u32[]{:S(2)}) copy-start(bf16[128,144]{0,1:T(8,128)(2,1)} %param.7) | copy-start | bytes 110596
  15.1 905.1 %all-to-all-start = ((bf16[8,576,2048]{2,1,0:T(8,128)(2,1)}), bf16[8,576,2048]{2,1,0:T(8,128)(2,1)}, u32[]{:S(2)}, u32[]{:S(2)}) async-start(bf16[8,576,2048]{2,1,0:T(8,128)(2,1)} %stack.2), calls=%async_computation | async-start | bytes 37748736 | tf_op jit(solution)/shard_map/all_to_all | solution.py:12
  26.7 444.1 %all-gather.3.cloned.1.call-start = ((), (), s32[]{:S(2)}) async-start(), calls=%async_computation.2 | async-start | bytes 1216512 | tf_op jit(solution)/shard_map/all_gather | solution.py:21
  27.4 601.6 %all-reduce.3.cloned.1.call-start = ((), (), s32[]{:S(2)}) async-start(), calls=%async_computation.3 | async-start | bytes 5308416 | tf_op jit(solution)/shard_map/psum | solution.py:26
  474.1 446.1 %all-reduce.5.cloned.1.call-start = ((), (), s32[]{:S(2)}) async-start(), calls=%async_computation.4 | async-start | bytes 4718592 | tf_op jit(solution)/shard_map/psum | solution.py:34
  633.1 0.7 copy-start.3
  633.1 288.3 %copy-start.1 = (bf16[4608,128]{1,0:T(8,128)(2,1)S(1)}, bf16[4608,128]{1,0:T(8,128)(2,1)}, u32[]{:S(2)}) copy-start(bf16[4608,128]{1,0:T(8,128)(2,1)} %all-gather.3.cloned.1.call-done) | copy-start | bytes 3538948
  633.1 288.3 %copy-start.4 = (f32[2048]{0:T(1024)S(1)}, f32[2048]{0:T(1024)}, u32[]{:S(2)}) copy-start(f32[2048]{0:T(1024)} %param.10) | copy-start | bytes 24580
  633.1 403.8 %all-gather.5.cloned.1.call-start = ((), (), s32[]{:S(2)}) async-start(), calls=%async_computation.5 | async-start | bytes 4718592 | tf_op jit(solution)/shard_map/all_gather | solution.py:63
  932.1 258.6 %reduce-scatter.2.cloned.1.call-start = ((), (), s32[]{:S(2)}) async-start(), calls=%async_computation.6 | async-start | bytes 2703360 | tf_op jit(solution)/shard_map/reduce_scatter | solution.py:67
  1044.1 146.6 %copy-start.5 = (f32[576]{0:T(1024)S(1)}, f32[576]{0:T(1024)}, u32[]{:S(2)}) copy-start(f32[576]{0:T(1024)} %param.11) | copy-start | bytes 6916
Sparse Core Ops, SparseCore 0:
  29.3 441.4 all-gather.2
  474.2 154.7 all-reduce.2
  633.2 286.8 all-reduce.4
  932.2 104.6 all-gather.4
  1044.2 146.4 reduce-scatter.1
